TPU v7x, 32 devices: a whole 2x2x4 slice. The times are simulated.
32 devices in a mesh: db: 8 (over z, x), pb: 4 (over y, core).
Axes of the slice: x: 2, y: 2, z: 4, core: 2. Of those that a mesh axis runs over, the one named last changes fastest.
Arguments:
- queries: bfloat16 [256, 4096], P('pb'), may hold values from -6 to 6
- database: bfloat16 [8192, 4096], P(('db', 'pb')), may hold values from -6 to 6
- slopes: int32 [5], replicated, may hold values from 1 to 6, as said below
Outputs:
- match_score: float32 [256, 8192], P(None, ('db', 'pb'))
Inputs may be any that keep to these rules, and one draw needn't show every extreme that they name: `slopes`: every slope lies in 1 to 6; one of them is 6 and one is 1.
All inputs are finite; a program needn't handle non-finite values.
Results may differ from a plain program's by a relative error of at most 0.0003.
Values may be sent and summed in bfloat16 or wider, within the bound.
A program may use at most 64 MiB of HBM per device.

v0:
```python
import jax
import jax.numpy as jnp
from jax import lax
from jax.sharding import PartitionSpec as P

SEQ = 20
RADIUS = 5
SLOPES = 5
SMAX = 6
variance_floor = 0.25


def padded_2(value, sides, width):
    for axis, dim in sides:
        count, length = (lax.axis_size(axis), value.shape[dim])
        up = [(i, (i + 1) % count) for i in range(count - 1)]
        down = [(j, i) for i, j in up]
        last = lax.slice_in_dim(value, length - width, length, axis=dim)
        leading = lax.slice_in_dim(value, 0, width, axis=dim)
        before = lax.ppermute(last, axis, up)
        after = lax.ppermute(leading, axis, down)
        value = jnp.concatenate([before, value, after], axis=dim)
    return value


def from_behind(value, axis, steps):
    count = lax.axis_size(axis)
    leading, last = (max(0, -steps), min(count, count - steps))
    return lax.ppermute(value, axis, [(source, source + steps) for source in range(leading, last)])


def band_mask(first_frame, frame_count, band_total):
    frame_ids = first_frame + jnp.arange(frame_count, dtype=jnp.int32)
    inside = jnp.logical_and(frame_ids >= 0, frame_ids < band_total)
    return inside.astype(jnp.float32)[None, :]


def contrast(extended, validity):
    out_width = extended.shape[1] - 2 * RADIUS
    masked = extended * validity
    squared = masked * masked
    first_sum = masked[:, :out_width]
    second_sum = squared[:, :out_width]
    counted = validity[:, :out_width]
    for offset in range(1, 2 * RADIUS + 1):
        first_sum = first_sum + masked[:, offset : offset + out_width]
        second_sum = second_sum + squared[:, offset : offset + out_width]
        counted = counted + validity[:, offset : offset + out_width]
    counted = jnp.maximum(counted, 1.0)
    average = first_sum / counted
    spread = second_sum / counted - average * average
    center = extended[:, RADIUS : RADIUS + out_width]
    keeper = validity[:, RADIUS : RADIUS + out_width]
    return keeper * (center - average) / jnp.sqrt(jnp.maximum(spread, variance_floor))


def lagged(field, steps, slope):
    col_pad = steps * SMAX
    padded = jnp.pad(field, ((steps, 0), (col_pad, 0)))
    begin = col_pad - steps * slope
    return lax.dynamic_slice(padded, (jnp.int32(0), begin), field.shape)


def window_sum(field, slope):
    powers = [field]
    stride = 1
    while 2 * stride <= SEQ:
        powers.append(powers[-1] + lagged(powers[-1], stride, slope))
        stride = stride * 2
    summed = None
    filled = 0
    for level in reversed(range(len(powers))):
        if SEQ >> level & 1:
            segment = powers[level] if filled == 0 else lagged(powers[level], filled, slope)
            summed = segment if summed is None else summed + segment
            filled = filled + (1 << level)
    return summed


def best_match(joined, slopes, reach):
    highest = None
    for member in range(SLOPES):
        summed = window_sum(joined, slopes[member])[:, reach:]
        highest = summed if highest is None else jnp.maximum(highest, summed)
    return highest * SEQ ** (-0.5)


def on_device(queries, database, slopes):
    frames = database.shape[0]
    scale = database.shape[1] ** (-0.5)
    reach = SMAX * (SEQ - 1)
    band_total = frames * lax.axis_size(("db", "pb"))
    similarity = (
        lax.dot_general(
            lax.all_gather(queries, "pb", axis=0, tiled=True),
            database,
            (((1,), (1,)), ((), ())),
            preferred_element_type=jnp.float32,
        )
        * scale
    )
    anchor = lax.axis_index(("db", "pb")) * frames
    extended = padded_2(similarity, ((("db", "pb"), 1),), RADIUS)
    normed = contrast(extended, band_mask(anchor - RADIUS, frames + 2 * RADIUS, band_total))
    carried = from_behind(normed[:, frames - reach :], ("db", "pb"), 1)
    joined = jnp.concatenate([carried, normed], axis=1)
    return best_match(joined, slopes, reach)


def solution(mesh):
    placed = (P("pb", None), P(("db", "pb"), None), P())
    return jax.shard_map(
        on_device, mesh=mesh, in_specs=placed, out_specs=P(None, ("db", "pb")), check_vma=False
    )
```

profile of v0, /device:TPU:7, one launch (start us, length us, event | category | flops | bytes accessed | tf_op | source)
XLA Modules:
  0.0 78.5 jit_solution(4593972485175373865)
XLA Ops:
  6.5 0.0 copy-start
  6.5 0.0 all-gather.2.cloned.1.call-start
  6.5 0.7 all-gather.2.cloned.1.call-update
  7.3 0.1 fusion.44
  7.4 24.8 %all-gather.2.cloned.1.call-done = bf16[256,4096]{1,0:T(8,128)(2,1)} async-done(((bf16[64,4096]{1,0:T(8,128)(2,1)}), bf16[256,4096]{1,0:T(8,128)(2,1)}) %all-gather.2.cloned.1.call-update) | async-done | bytes 2097168 | tf_op jit(solution)/shard_map/all_gather | solution.py:95
  32.2 0.0 copy-done
  32.2 2.3 %convolution_multiply_fusion = f32[256,256]{0,1:T(8,128)S(1)} fusion(bf16[256,4096]{1,0:T(8,128)(2,1)} %all-gather.2.cloned.1.call-done, bf16[256,4096]{1,0:T(8,128)(2,1)S(1)} %copy-done), kind=kOutput, calls=%fused_computation | convolution fusion | flops 536936448 | bytes 4456448 | tf_op jit(solution)/shard_map/dot_general | solution.py:94
  34.6 4.2 %collective-permute-start = (f32[256,5]{0,1:T(8,128)S(1)}, f32[256,5]{0,1:T(8,128)S(1)}, u32[]{:S(2)}, u32[]{:S(2)}) collective-permute-start(f32[256,5]{0,1:T(8,128)S(1)} %get-tuple-element.12), channel_id=1, source_target_pairs={{0,1},{1,2},{2,3},{3,4},{4,5},{5,6},{6,7},{7,8},{8,9},{9,10},{10,1... | collective-permute-start | bytes 15368 | tf_op jit(solution)/shard_map/ppermute | solution.py:20
  38.7 1.9 %collective-permute-start.1 = (f32[256,5]{0,1:T(8,128)S(1)}, f32[256,5]{0,1:T(8,128)S(1)}, u32[]{:S(2)}, u32[]{:S(2)}) collective-permute-start(f32[256,5]{0,1:T(8,128)S(1)} %get-tuple-element.13), channel_id=1, source_target_pairs={{1,0},{2,1},{3,2},{4,3},{5,4},{6,5},{7,6},{8,7},{9,8},{10,9},{11,1... | collective-permute-start | bytes 15368 | tf_op jit(solution)/shard_map/ppermute | solution.py:21
  40.7 0.0 collective-permute-done
  40.7 4.8 %collective-permute-done.1 = f32[256,5]{0,1:T(8,128)S(1)} collective-permute-done((f32[256,5]{0,1:T(8,128)S(1)}, f32[256,5]{0,1:T(8,128)S(1)}, u32[]{:S(2)}, u32[]{:S(2)}) %collective-permute-start.1) | collective-permute-done | bytes 5152 | tf_op jit(solution)/shard_map/ppermute | solution.py:21
  45.5 0.1 fusion.42
  45.6 0.0 copy-start.1
  45.6 0.5 fusion.34
  46.2 1.9 %collective-permute-start.2 = (f32[256,114]{0,1:T(8,128)S(1)}, f32[256,114]{0,1:T(8,128)S(1)}, u32[]{:S(2)}, u32[]{:S(2)}) collective-permute-start(f32[256,114]{0,1:T(8,128)S(1)} %slice.220), channel_id=1, source_target_pairs={{0,1},{1,2},{2,3},{3,4},{4,5},{5,6},{6,7},{7,8},{8,9},{9,10},{10,1... | collective-permute-start | bytes 350216 | tf_op jit(solution)/shard_map/ppermute | solution.py:29
  48.1 0.0 copy-done.1
  48.2 0.7 fusion.45
  67.1 0.0 collective-permute-done.2
  67.1 0.7 fusion.14
  67.8 0.2 fusion.4
  68.0 0.2 fusion.9
  68.2 0.3 fusion.2
  68.5 0.2 fusion.7
  68.7 0.2 fusion.8
  68.9 0.3 fusion
  69.2 0.2 fusion.5
  69.4 0.2 fusion.6
  69.6 1.2 %fusion.21 = f32[256,256]{0,1:T(8,128)S(1)} fusion(s32[]{:T(128)S(6)} %add.489, f32[256,370]{0,1:T(8,128)S(1)} %fusion.5, s32[]{:T(128)S(6)} %add.491, f32[256,370]{0,1:T(8,128)S(1)} %fusion.6, s32[]{:T(128)S(6)} %add.493, f32[256,370]{0,1:T(8,128)S(1)} %fusion.7, s32[]{:T(128)S(6)} %add.495, f32[256,370]{0,1:T(8,128)S(1)} %fusion.8, s32[]{:T(128)S(6)} %add.497, ...), kind=kLoop, calls=%fused_computation.49 | loop fusion | flops 983040 | bytes 5423144 | tf_op jit(solution)/shard_map/mul | solution.py:85
  70.8 0.8 %copy.4 = f32[256,256]{1,0:T(8,128)} copy(f32[256,256]{0,1:T(8,128)S(1)} %fusion.21) | data formatting | bytes 524288 | tf_op jit(solution)/shard_map/mul | solution.py:85
  (5 shorter events, 0.1 us)
Async XLA Ops:
  6.5 25.7 %copy-start = (bf16[256,4096]{1,0:T(8,128)(2,1)S(1)}, bf16[256,4096]{1,0:T(8,128)(2,1)}, u32[]{:S(2)}) copy-start(bf16[256,4096]{1,0:T(8,128)(2,1)} %param.4) | copy-start | bytes 6291460
  6.5 25.7 %all-gather.2.cloned.1.call-start = ((), (), s32[]{:S(2)}) async-start(), calls=%async_computation | async-start | bytes 2621440 | tf_op jit(solution)/shard_map/all_gather | solution.py:95
  34.6 6.1 %collective-permute-start = (f32[256,5]{0,1:T(8,128)S(1)}, f32[256,5]{0,1:T(8,128)S(1)}, u32[]{:S(2)}, u32[]{:S(2)}) collective-permute-start(f32[256,5]{0,1:T(8,128)S(1)} %get-tuple-element.12), channel_id=1, source_target_pairs={{0,1},{1,2},{2,3},{3,4},{4,5},{5,6},{6,7},{7,8},{8,9},{9,10},{10,1... | collective-permute-start | bytes 15368 | tf_op jit(solution)/shard_map/ppermute | solution.py:20
  38.7 6.8 %collective-permute-start.1 = (f32[256,5]{0,1:T(8,128)S(1)}, f32[256,5]{0,1:T(8,128)S(1)}, u32[]{:S(2)}, u32[]{:S(2)}) collective-permute-start(f32[256,5]{0,1:T(8,128)S(1)} %get-tuple-element.13), channel_id=1, source_target_pairs={{1,0},{2,1},{3,2},{4,3},{5,4},{6,5},{7,6},{8,7},{9,8},{10,9},{11,1... | collective-permute-start | bytes 15368 | tf_op jit(solution)/shard_map/ppermute | solution.py:21
  45.6 2.5 %copy-start.1 = (s32[5]{0:T(128)S(1)}, s32[5]{0:T(128)}, u32[]{:S(2)}) copy-start(s32[5]{0:T(128)} %param.5) | copy-start | bytes 64
  46.2 20.9 %collective-permute-start.2 = (f32[256,114]{0,1:T(8,128)S(1)}, f32[256,114]{0,1:T(8,128)S(1)}, u32[]{:S(2)}, u32[]{:S(2)}) collective-permute-start(f32[256,114]{0,1:T(8,128)S(1)} %slice.220), channel_id=1, source_target_pairs={{0,1},{1,2},{2,3},{3,4},{4,5},{5,6},{6,7},{7,8},{8,9},{9,10},{10,1... | collective-permute-start | bytes 350216 | tf_op jit(solution)/shard_map/ppermute | solution.py:29
Sparse Core Ops, SparseCore 0:
  8.9 23.2 all-gather.1
where the time goes:
time: 78.9 us; the launch traced here: 78.5 us
  between operations  31.8 us (40%)
  waiting for transfers between devices  30.4 us (39%)
  starting transfers between devices  8.05 us (10%)
  other arithmetic  4.36 us (6%)
  matrix products  2.33 us (3%)
  local copies, waits for them, and re-layouts  1.52 us (2%)
    all_gather x1, waiting for transfers between devices, on_device(): lax.all_gather(queries, 'pb', axis=0, tiled=True)  24.8 us
    ppermute x1, waiting for transfers between devices, padded_2(): after = lax.ppermute(leading, axis, down)  4.81 us
    ppermute x1, starting transfers between devices, padded_2(): before = lax.ppermute(last, axis, up)  4.18 us
    add x9, other arithmetic, window_sum(): powers.append(powers[-1] + lagged(powers[-1], stride, slope))  2.43 us
    dot_general x1, matrix products, on_device(): lax.dot_general(lax.all_gather(queries, 'pb', axis=0, tiled=True), databa...  2.33 us
    ppermute x1, starting transfers between devices, from_behind(): lax.ppermute(value, axis, [(source, source + steps) for source in range(l...  1.94 us
    ppermute x1, starting transfers between devices, padded_2(): after = lax.ppermute(leading, axis, down)  1.92 us
  transfers between devices with their start and end apart: 4, of which 2 were waited for; matrix products, arithmetic and copies ran while one was open for 1% of the time, Pallas kernels for 0%

commit v1 on v0

--- a/solution.py
+++ b/solution.py
@@ -8,6 +8,25 @@
 SLOPES = 5
 SMAX = 6
 variance_floor = 0.25
+
+
+def ring_gather(x, axis, dim):
+    size, mine, rows = (lax.axis_size(axis), lax.axis_index(axis), x.shape[dim])
+    forward = [(i, (i + 1) % size) for i in range(size)]
+    behind = [(i, (i - 1) % size) for i in range(size)]
+    out = jnp.zeros((*x.shape[:dim], size * rows, *x.shape[dim + 1 :]), x.dtype)
+    out = lax.dynamic_update_slice_in_dim(out, x, mine * rows, axis=dim)
+    from_left = from_right = x
+    halfway = size // 2
+    for step in range(1, halfway + 1):
+        from_left = lax.ppermute(from_left, axis, forward)
+        out = lax.dynamic_update_slice_in_dim(out, from_left, (mine - step) % size * rows, axis=dim)
+        if step < size - halfway:
+            from_right = lax.ppermute(from_right, axis, behind)
+            out = lax.dynamic_update_slice_in_dim(
+                out, from_right, (mine + step) % size * rows, axis=dim
+            )
+    return out
 
 
 def padded_2(value, sides, width):
@@ -92,7 +111,7 @@
     band_total = frames * lax.axis_size(("db", "pb"))
     similarity = (
         lax.dot_general(
-            lax.all_gather(queries, "pb", axis=0, tiled=True),
+            ring_gather(queries, "pb", 0),
             database,
             (((1,), (1,)), ((), ())),
             preferred_element_type=jnp.float32,

time: 78.9 us -> 62.9 us (0.80)
  the two profiles are of different devices: /device:TPU:7 before, /device:TPU:0 now
where the time goes in v1:
time: 62.9 us; the launch traced here: 62.4 us
  between operations  18.7 us (30%)
  starting transfers between devices  15 us (24%)
  waiting for transfers between devices  14.5 us (23%)
  local copies, waits for them, and re-layouts  7.49 us (12%)
  other arithmetic  4.34 us (7%)
  matrix products  2.33 us (4%)
    ppermute x2, waiting for transfers between devices, ring_gather(): from_left = lax.ppermute(from_left, axis, forward)  10.8 us
    ppermute x1, starting transfers between devices, padded_2(): before = lax.ppermute(last, axis, up)  4.35 us
    ppermute x1, starting transfers between devices, from_behind(): lax.ppermute(value, axis, [(source, source + steps) for source in range(l...  4.31 us
    ppermute x1, waiting for transfers between devices, padded_2(): after = lax.ppermute(leading, axis, down)  3.71 us
    ppermute x2, starting transfers between devices, ring_gather(): from_left = lax.ppermute(from_left, axis, forward)  3.02 us
    add x9, other arithmetic, window_sum(): powers.append(powers[-1] + lagged(powers[-1], stride, slope))  2.41 us
    dot_general x1, matrix products, on_device(): lax.dot_general(ring_gather(queries, 'pb', 0), database, (((1,), (1,)), (...  2.33 us
    ppermute x1, starting transfers between devices, ring_gather(): from_right = lax.ppermute(from_right, axis, behind)  2.01 us
  transfers between devices with their start and end apart: 6, of which 3 were waited for; matrix products, arithmetic and copies ran while one was open for 9% of the time, Pallas kernels for 0%

profile of v1, /device:TPU:0, one launch (start us, length us, event | category | flops | bytes accessed | tf_op | source)
XLA Modules:
  0.0 62.4 jit_solution(13298797206060666680)
XLA Ops:
  0.0 0.0 copy-start
  0.0 0.0 copy-start.1
  0.0 0.5 collective-permute-start
  0.5 2.0 %collective-permute-start.1 = (bf16[64,4096]{1,0:T(8,128)(2,1)}, bf16[64,4096]{1,0:T(8,128)(2,1)}, u32[]{:S(2)}, u32[]{:S(2)}) collective-permute-start(bf16[64,4096]{1,0:T(8,128)(2,1)} %param.3), channel_id=1, source_target_pairs={{0,3},{1,0},{2,1},{3,2},{4,7},{5,4},{6,5},{7,6},{8,11},{9,8},{10,9... | collective-permute-start | bytes 1572872 | tf_op jit(solution)/shard_map/ppermute | solution.py:25
  2.5 1.6 %broadcast_in_dim.4 = bf16[256,4096]{1,0:T(8,128)(2,1)} broadcast(bf16[]{:T(256)} %constant.156.clone.1), dimensions={} | broadcast | bytes 2097154 | tf_op jit(solution)/shard_map/broadcast_in_dim | solution.py:17
  4.1 0.0 copy-done.1
  4.1 0.8 %constant_dynamic-update-slice_fusion.3 = bf16[256,4096]{1,0:T(8,128)(2,1)} fusion(bf16[256,4096]{1,0:T(8,128)(2,1)} %broadcast_in_dim.4, bf16[64,4096]{1,0:T(8,128)(2,1)S(1)} %copy-done.1, s32[]{:T(128)S(6)} %select_n.102), kind=kLoop, calls=%fused_computation.87 | loop fusion | bytes 1048580 | tf_op jit(solution)/shard_map/dynamic_update_slice | solution.py:18
  4.9 0.1 fusion.44
  5.0 7.5 %collective-permute-done = bf16[64,4096]{1,0:T(8,128)(2,1)S(1)} collective-permute-done((bf16[64,4096]{1,0:T(8,128)(2,1)}, bf16[64,4096]{1,0:T(8,128)(2,1)S(1)}, u32[]{:S(2)}, u32[]{:S(2)}) %collective-permute-start) | collective-permute-done | bytes 524320 | tf_op jit(solution)/shard_map/ppermute | solution.py:22
  12.5 2.6 %collective-permute-start.2 = (bf16[64,4096]{1,0:T(8,128)(2,1)S(1)}, bf16[64,4096]{1,0:T(8,128)(2,1)S(1)}, u32[]{:S(2)}, u32[]{:S(2)}) collective-permute-start(bf16[64,4096]{1,0:T(8,128)(2,1)S(1)} %collective-permute-done), channel_id=1, source_target_pairs={{0,1},{1,2},{2,3},{3,0},{4,5},{5,6},{6,7},{7,4},{8,9},{9,10},{10,1... | collective-permute-start | bytes 1572872 | tf_op jit(solution)/shard_map/ppermute | solution.py:22
  15.1 0.8 %constant_dynamic-update-slice_fusion.2 = bf16[256,4096]{1,0:T(8,128)(2,1)} fusion(bf16[256,4096]{1,0:T(8,128)(2,1)} %constant_dynamic-update-slice_fusion.3, bf16[64,4096]{1,0:T(8,128)(2,1)S(1)} %collective-permute-done, s32[]{:T(128)S(6)} %select_n.104), kind=kLoop, calls=%fused_computation.86 | loop fusion | bytes 1048580 | tf_op jit(solution)/shard_map/dynamic_update_slice | solution.py:23
  15.9 0.0 collective-permute-done.1
  15.9 1.9 %constant_dynamic-update-slice_fusion.1 = bf16[256,4096]{1,0:T(8,128)(2,1)} fusion(bf16[256,4096]{1,0:T(8,128)(2,1)} %constant_dynamic-update-slice_fusion.2, bf16[64,4096]{1,0:T(8,128)(2,1)} %collective-permute-done.1, s32[]{:T(128)S(6)} %select_n.106), kind=kLoop, calls=%fused_computation.85 | loop fusion | bytes 1048580 | tf_op jit(solution)/shard_map/dynamic_update_slice | solution.py:26
  17.8 3.3 %collective-permute-done.2 = bf16[64,4096]{1,0:T(8,128)(2,1)S(1)} collective-permute-done((bf16[64,4096]{1,0:T(8,128)(2,1)S(1)}, bf16[64,4096]{1,0:T(8,128)(2,1)S(1)}, u32[]{:S(2)}, u32[]{:S(2)}) %collective-permute-start.2) | collective-permute-done | bytes 524320 | tf_op jit(solution)/shard_map/ppermute | solution.py:22
  21.1 0.9 %constant_dynamic-update-slice_fusion = bf16[256,4096]{1,0:T(8,128)(2,1)} fusion(bf16[256,4096]{1,0:T(8,128)(2,1)} %constant_dynamic-update-slice_fusion.1, bf16[64,4096]{1,0:T(8,128)(2,1)S(1)} %collective-permute-done.2, s32[]{:T(128)S(6)} %select_n.108), kind=kLoop, calls=%fused_computation.84 | loop fusion | bytes 1048580 | tf_op jit(solution)/shard_map/dynamic_update_slice | solution.py:23
  22.0 0.0 copy-done
  22.0 2.3 %convolution_multiply_fusion = f32[256,256]{0,1:T(8,128)S(1)} fusion(bf16[256,4096]{1,0:T(8,128)(2,1)} %constant_dynamic-update-slice_fusion, bf16[256,4096]{1,0:T(8,128)(2,1)S(1)} %copy-done), kind=kOutput, calls=%fused_computation | convolution fusion | flops 536936448 | bytes 4456448 | tf_op jit(solution)/shard_map/dot_general | solution.py:113
  24.3 4.3 %collective-permute-start.3 = (f32[256,5]{0,1:T(8,128)S(1)}, f32[256,5]{0,1:T(8,128)S(1)}, u32[]{:S(2)}, u32[]{:S(2)}) collective-permute-start(f32[256,5]{0,1:T(8,128)S(1)} %get-tuple-element.12), channel_id=1, source_target_pairs={{0,1},{1,2},{2,3},{3,4},{4,5},{5,6},{6,7},{7,8},{8,9},{9,10},{10,1... | collective-permute-start | bytes 15368 | tf_op jit(solution)/shard_map/ppermute | solution.py:39
  28.7 1.3 %collective-permute-start.4 = (f32[256,5]{0,1:T(8,128)S(1)}, f32[256,5]{0,1:T(8,128)S(1)}, u32[]{:S(2)}, u32[]{:S(2)}) collective-permute-start(f32[256,5]{0,1:T(8,128)S(1)} %get-tuple-element.13), channel_id=1, source_target_pairs={{1,0},{2,1},{3,2},{4,3},{5,4},{6,5},{7,6},{8,7},{9,8},{10,9},{11,1... | collective-permute-start | bytes 15368 | tf_op jit(solution)/shard_map/ppermute | solution.py:40
  30.0 0.0 collective-permute-done.3
  30.0 3.7 %collective-permute-done.4 = f32[256,5]{0,1:T(8,128)S(1)} collective-permute-done((f32[256,5]{0,1:T(8,128)S(1)}, f32[256,5]{0,1:T(8,128)S(1)}, u32[]{:S(2)}, u32[]{:S(2)}) %collective-permute-start.4) | collective-permute-done | bytes 5152 | tf_op jit(solution)/shard_map/ppermute | solution.py:40
  33.7 0.1 fusion.42
  33.8 0.0 copy-start.2
  33.8 0.5 fusion.34
  34.4 4.3 %collective-permute-start.5 = (f32[256,114]{0,1:T(8,128)S(1)}, f32[256,114]{0,1:T(8,128)S(1)}, u32[]{:S(2)}, u32[]{:S(2)}) collective-permute-start(f32[256,114]{0,1:T(8,128)S(1)} %slice.220), channel_id=1, source_target_pairs={{0,1},{1,2},{2,3},{3,4},{4,5},{5,6},{6,7},{7,8},{8,9},{9,10},{10,1... | collective-permute-start | bytes 350216 | tf_op jit(solution)/shard_map/ppermute | solution.py:48
  38.7 0.0 copy-done.2
  38.7 0.6 %fusion.45 = (s32[1]{0:T(128)}, s32[1]{0:T(128)}, s32[1]{0:T(128)}, s32[1]{0:T(128)}, s32[1]{0:T(128)}) fusion(s32[5]{0:T(128)S(1)} %copy-done.2), kind=kLoop, calls=%fused_computation.108 | loop fusion | bytes 40 | tf_op jit(solution)/shard_map/slice | solution.py:102
  57.8 0.0 collective-permute-done.5
  57.9 0.6 %fusion.14 = (f32[256,370]{0,1:T(8,128)S(1)}, f32[256,370]{0,1:T(8,128)S(1)}, f32[256,370]{0,1:T(8,128)S(1)}, f32[256,370]{0,1:T(8,128)S(1)}, f32[256,370]{0,1:T(8,128)S(1)}) fusion(f32[256,370]{0,1:T(8,128)S(1)} %pad_maximum_fusion, s32[]{:T(128)S(6)} %select_n.129, s32[]{:T(128)S(6)} %select_n.124, s32[]{:T(128)S(6)} %select_n.119, s32[]{:T(128)S(6)} %select_n.114, ...), kind=kLoop, calls=%fused_computation.40 | loop fusion | flops 473600 | bytes 2273300 | tf_op jit(solution)/shard_map/add | solution.py:87
  58.5 0.3 fusion.2
  58.9 0.2 fusion.8
  59.1 0.2 fusion.7
  59.3 0.3 fusion
  59.6 0.2 fusion.6
  59.8 0.2 fusion.5
  60.0 0.2 fusion.4
  60.2 0.2 fusion.9
  60.3 1.2 %fusion.21 = f32[256,256]{0,1:T(8,128)S(1)} fusion(s32[]{:T(128)S(6)} %add.524, f32[256,370]{0,1:T(8,128)S(1)} %fusion.5, s32[]{:T(128)S(6)} %add.526, f32[256,370]{0,1:T(8,128)S(1)} %fusion.6, s32[]{:T(128)S(6)} %add.528, f32[256,370]{0,1:T(8,128)S(1)} %fusion.7, s32[]{:T(128)S(6)} %add.530, f32[256,370]{0,1:T(8,128)S(1)} %fusion.8, s32[]{:T(128)S(6)} %add.532, ...), kind=kLoop, calls=%fused_computation.49 | loop fusion | flops 983040 | bytes 5423144 | tf_op jit(solution)/shard_map/mul | solution.py:104
  61.5 0.8 %copy.4 = f32[256,256]{1,0:T(8,128)} copy(f32[256,256]{0,1:T(8,128)S(1)} %fusion.21) | data formatting | bytes 524288 | tf_op jit(solution)/shard_map/mul | solution.py:104
  (5 shorter events, 0.1 us)
Async XLA Ops:
  0.0 22.0 %copy-start = (bf16[256,4096]{1,0:T(8,128)(2,1)S(1)}, bf16[256,4096]{1,0:T(8,128)(2,1)}, u32[]{:S(2)}) copy-start(bf16[256,4096]{1,0:T(8,128)(2,1)} %param.4) | copy-start | bytes 6291460
  0.0 4.1 %copy-start.1 = (bf16[64,4096]{1,0:T(8,128)(2,1)S(1)}, bf16[64,4096]{1,0:T(8,128)(2,1)}, u32[]{:S(2)}) copy-start(bf16[64,4096]{1,0:T(8,128)(2,1)} %param.3) | copy-start | bytes 1572868
  0.0 12.5 %collective-permute-start = (bf16[64,4096]{1,0:T(8,128)(2,1)}, bf16[64,4096]{1,0:T(8,128)(2,1)S(1)}, u32[]{:S(2)}, u32[]{:S(2)}) collective-permute-start(bf16[64,4096]{1,0:T(8,128)(2,1)} %param.3), channel_id=1, source_target_pairs={{0,1},{1,2},{2,3},{3,0},{4,5},{5,6},{6,7},{7,4},{8,9},{9,10},{10,1... | collective-permute-start | bytes 1572872 | tf_op jit(solution)/shard_map/ppermute | solution.py:22
  0.5 15.5 %collective-permute-start.1 = (bf16[64,4096]{1,0:T(8,128)(2,1)}, bf16[64,4096]{1,0:T(8,128)(2,1)}, u32[]{:S(2)}, u32[]{:S(2)}) collective-permute-start(bf16[64,4096]{1,0:T(8,128)(2,1)} %param.3), channel_id=1, source_target_pairs={{0,3},{1,0},{2,1},{3,2},{4,7},{5,4},{6,5},{7,6},{8,11},{9,8},{10,9... | collective-permute-start | bytes 1572872 | tf_op jit(solution)/shard_map/ppermute | solution.py:25
  12.5 8.6 %collective-permute-start.2 = (bf16[64,4096]{1,0:T(8,128)(2,1)S(1)}, bf16[64,4096]{1,0:T(8,128)(2,1)S(1)}, u32[]{:S(2)}, u32[]{:S(2)}) collective-permute-start(bf16[64,4096]{1,0:T(8,128)(2,1)S(1)} %collective-permute-done), channel_id=1, source_target_pairs={{0,1},{1,2},{2,3},{3,0},{4,5},{5,6},{6,7},{7,4},{8,9},{9,10},{10,1... | collective-permute-start | bytes 1572872 | tf_op jit(solution)/shard_map/ppermute | solution.py:22
  24.3 5.7 %collective-permute-start.3 = (f32[256,5]{0,1:T(8,128)S(1)}, f32[256,5]{0,1:T(8,128)S(1)}, u32[]{:S(2)}, u32[]{:S(2)}) collective-permute-start(f32[256,5]{0,1:T(8,128)S(1)} %get-tuple-element.12), channel_id=1, source_target_pairs={{0,1},{1,2},{2,3},{3,4},{4,5},{5,6},{6,7},{7,8},{8,9},{9,10},{10,1... | collective-permute-start | bytes 15368 | tf_op jit(solution)/shard_map/ppermute | solution.py:39
  28.7 5.0 %collective-permute-start.4 = (f32[256,5]{0,1:T(8,128)S(1)}, f32[256,5]{0,1:T(8,128)S(1)}, u32[]{:S(2)}, u32[]{:S(2)}) collective-permute-start(f32[256,5]{0,1:T(8,128)S(1)} %get-tuple-element.13), channel_id=1, source_target_pairs={{1,0},{2,1},{3,2},{4,3},{5,4},{6,5},{7,6},{8,7},{9,8},{10,9},{11,1... | collective-permute-start | bytes 15368 | tf_op jit(solution)/shard_map/ppermute | solution.py:40
  33.8 4.9 %copy-start.2 = (s32[5]{0:T(128)S(1)}, s32[5]{0:T(128)}, u32[]{:S(2)}) copy-start(s32[5]{0:T(128)} %param.5) | copy-start | bytes 64
  34.4 23.5 %collective-permute-start.5 = (f32[256,114]{0,1:T(8,128)S(1)}, f32[256,114]{0,1:T(8,128)S(1)}, u32[]{:S(2)}, u32[]{:S(2)}) collective-permute-start(f32[256,114]{0,1:T(8,128)S(1)} %slice.220), channel_id=1, source_target_pairs={{0,1},{1,2},{2,3},{3,4},{4,5},{5,6},{6,7},{7,8},{8,9},{9,10},{10,1... | collective-permute-start | bytes 350216 | tf_op jit(solution)/shard_map/ppermute | solution.py:48
